TPU v7x, 256 devices: a whole 4x4x8 slice. The times are simulated.
256 devices in a mesh: rows: 64 (over x_hi, z, y), outs: 4 (over x_lo, core).
Axes of the slice: x: 4 (x_hi: 2, x_lo: 2; x = x_hi * 2 + x_lo), y: 4, z: 8, core: 2. Of those that a mesh axis runs over, the one named last changes fastest.
Arguments:
- grads: bfloat16 [393216, 1024], P('rows', 'outs'), may hold values from -6 to 6
- projection: bfloat16 [1024, 8], replicated, may hold values from -0.1875 to 0.1875
- bins: int32 [393216, 256], P('rows'), may hold values from 0 to 127
- leaf: int32 [393216], P('rows'), may hold values from 0 to 3
Outputs:
- histogram: float32 [64, 4, 4, 8, 128], P('rows', 'outs')
All inputs are finite; a program needn't handle non-finite values.
Results may differ from a plain program's by a relative error of at most 0.0029.
Values may be sent and summed in bfloat16 or wider, within the bound.
A program may use at most 64 MiB of HBM per device.

v0:
```python
import math

import jax
import jax.numpy as jnp
from jax import lax
from jax.sharding import PartitionSpec as P

SK = 8
BINS = 128
LEAVES = 4


def leaf_weights(sketch, leaf):
    leaf_hot = (leaf[:, None] == jnp.arange(LEAVES, dtype=jnp.int32)[None, :]).astype(jnp.bfloat16)
    return (leaf_hot[:, :, None] * sketch[:, None, :]).reshape(sketch.shape[0], LEAVES * SK)


def hist_terms(weights, columns, count):
    group = math.gcd(count, 8)
    blocks = count // group
    levels = jnp.arange(BINS, dtype=jnp.int32)

    def one_block(index):
        block_cols = lax.dynamic_slice_in_dim(columns, index * group, group, 1)
        onehot = (block_cols[:, :, None] == levels[None, None, :]).astype(jnp.bfloat16)
        return jnp.einsum("rc,rgb->gcb", weights, onehot, preferred_element_type=jnp.float32)

    result = lax.map(one_block, jnp.arange(blocks, dtype=jnp.int32))
    return result.reshape(count, 1, LEAVES, SK, BINS)


def local(grads, projection, bins, leaf):
    n_rows = lax.axis_size("rows")
    n_outs = lax.axis_size("outs")
    outs_index = lax.axis_index("outs")
    rows_here = grads.shape[0]
    features = bins.shape[1]
    block = features // n_outs
    share = block // n_rows
    scale = math.sqrt(LEAVES * BINS / (rows_here * n_rows))
    quarter = rows_here // n_outs
    gathered = lax.all_to_all(grads, "outs", split_axis=0, concat_axis=1, tiled=True)
    sketch = jnp.dot(gathered, projection, preferred_element_type=jnp.float32).astype(jnp.bfloat16)
    leaf_part = lax.dynamic_slice_in_dim(leaf, outs_index * quarter, quarter, 0)
    bins_part = lax.dynamic_slice_in_dim(bins, outs_index * quarter, quarter, 0)
    columns = jnp.transpose(
        bins_part.reshape(quarter, n_outs, n_rows, share), (0, 2, 1, 3)
    ).reshape(quarter, features)
    weights = leaf_weights(sketch, leaf_part)
    summed = lax.psum_scatter(
        hist_terms(weights, columns, share * lax.axis_size(("rows", "outs"))),
        ("rows", "outs"),
        scatter_dimension=0,
        tiled=True,
    )
    return summed * jnp.float32(scale)


def solution(mesh):
    placed = (P("rows", "outs"), P(), P("rows", None), P("rows"))
    return jax.shard_map(
        local,
        mesh=mesh,
        in_specs=placed,
        out_specs=P("rows", "outs", None, None, None),
        check_vma=False,
    )
```

profile of v0, /device:TPU:0, one launch (start us, length us, event | category | flops | bytes accessed | tf_op | source)
XLA Modules:
  0.0 1499.2 jit_solution(9718784403129750559)
XLA Ops:
  6.5 3.8 all-to-all-start
  13.9 3.1 copy.9
  17.0 3.6 copy.7
  23.5 23.8 %all-to-all-done = bf16[4,1536,256]{2,1,0:T(8,128)(2,1)S(1)} async-done(((bf16[4,1536,256]{2,1,0:T(8,128)(2,1)}), bf16[4,1536,256]{2,1,0:T(8,128)(2,1)S(1)}, u32[]{:S(2)}, u32[]{:S(2)}) %all-to-all-start) | async-done | bytes 3145760 | tf_op jit(solution)/shard_map/all_to_all | solution.py:42
  49.0 3.2 copy.8
  52.7 162.1 %while.11 = (s32[]{:T(128)}, f32[32,8,32,128]{3,2,1,0:T(8,128)}, s32[32]{0:T(128)S(1)}, s32[1536,256]{0,1:T(8,128)}, bf16[1536,8]{0,1:T(8,128)(2,1)S(1)}, /*inde...) while((s32[]{:T(128)}, f32[32,8,32,128]{3,2,1,0:T(8,128)}, ...), condition=%wide.region_1.2_spmd.clone, body=%wide.region_0.1_spmd.clone.sunk | while | flops 102285320 | bytes 315567 | solution.py:28
  59.8 3.0 fusion.18
  64.9 3.0 fusion.18
  69.9 3.0 fusion.18
  85.1 3.0 fusion.18
  90.2 3.0 fusion.18
  110.5 3.0 fusion.18
  115.5 3.0 fusion.18
  125.6 3.0 fusion.18
  130.7 3.0 fusion.18
  135.8 3.0 fusion.18
  140.8 3.0 fusion.18
  156.0 3.0 fusion.18
  161.1 3.0 fusion.18
  171.2 3.0 fusion.18
  176.3 3.0 fusion.18
  196.6 3.0 fusion.18
  211.7 3.0 fusion.18
  214.8 1276.2 %reduce-scatter.2.cloned.1.call-done = f32[1,1,4,8,128]{4,3,2,1,0:T(8,128)} async-done(((f32[256,1,4,8,128]{4,3,2,1,0:T(8,128)}), f32[1,1,4,8,128]{4,3,2,1,0:T(8,128)}) %reduce-scatter.2.cloned.1.call-update) | async-done | bytes 16400 | tf_op jit(solution)/shard_map/reduce_scatter | solution.py:50
  (93 shorter events, 100.8 us)
Async XLA Ops:
  6.5 45.6 %copy-start = (bf16[1024,8]{0,1:T(8,128)(2,1)S(1)}, bf16[1024,8]{0,1:T(8,128)(2,1)}, u32[]{:S(2)}) copy-start(bf16[1024,8]{0,1:T(8,128)(2,1)} %param.7) | copy-start | bytes 49156
  6.5 40.7 %all-to-all-start = ((bf16[4,1536,256]{2,1,0:T(8,128)(2,1)}), bf16[4,1536,256]{2,1,0:T(8,128)(2,1)S(1)}, u32[]{:S(2)}, u32[]{:S(2)}) async-start(bf16[4,1536,256]{2,1,0:T(8,128)(2,1)} %bitcast.33), calls=%async_computation | async-start | bytes 6291456 | tf_op jit(solution)/shard_map/all_to_all | solution.py:42
  10.4 1480.7 %reduce-scatter.2.cloned.1.call-start = ((), (), s32[]{:S(2)}) async-start(), calls=%async_computation.2 | async-start | bytes 4210688 | tf_op jit(solution)/shard_map/reduce_scatter | solution.py:50
  47.3 1.7 copy-start.1
Sparse Core Ops, SparseCore 0:
  214.9 1276.0 reduce-scatter.1
where the time goes:
time: 1500 us
  waiting for transfers between devices  1300 us (87%)
  matrix products  97.4 us (6%)
  local copies, waits for them, and re-layouts  63.3 us (4%)
  loops' own time  19.8 us (1%)
    reduce_scatter x1, waiting for transfers between devices, local(): lax.psum_scatter(hist_terms(weights, columns, share * lax.axis_size(('row...  1280 us
    dot_general x32, matrix products, one_block(): jnp.einsum('rc,rgb->gcb', weights, onehot, preferred_element_type=jnp.flo...  96.9 us
  transfers between devices with their start and end apart: 2, of which 2 were waited for; matrix products, arithmetic and copies ran while one was open for 1% of the time, Pallas kernels for 0%

commit v1 on v0

v1 whole, which is shorter than its diff:
```python
import functools
import math

import jax
import jax.numpy as jnp
from jax import lax
from jax.experimental import pallas as pl
from jax.experimental.pallas import tpu as pltpu
from jax.sharding import PartitionSpec as P

SK = 8
BINS = 128
LEAVES = 4
MESH = pl.DeviceIdType.MESH
BF = jnp.bfloat16
F32 = jnp.float32
NX, NZ, NY, NO = 2, 8, 4, 4
STEPS = NX * NZ
LAG = 2


def pieces(n_rows):
    r = lax.axis_index("rows")
    return r // (NZ * NY), (r // NY) % NZ, r % NY


def kernel(
    scale,
    grads, proj, bins, leaf,
    out,
    gbuf, pbuf, bbuf, lbuf, part, skin, skq, skr, sk16, bh, cc,
    fbuf, sbuf, rbuf1, s2, rbuf2,
    lsem, osem, qs_send, qs_recv, ag_send, ag_recv, y_send, y_recv, z_send, z_recv,
):
    x, z, y = pieces(NX * NZ * NY)
    o = lax.axis_index("outs")
    rows = bh.shape[1]
    quarter = rows // NO
    half = quarter // 2
    order = (2, 1, 3, 0)

    pcopy = pltpu.make_async_copy(proj, pbuf, lsem.at[8])
    pcopy.start()
    gcopies = []
    for i, d in enumerate(order):
        q = (o + d) % NO
        g = pltpu.make_async_copy(
            grads.at[pl.ds(pl.multiple_of(q * quarter, quarter), quarter), :], gbuf.at[i], lsem.at[i]
        )
        g.start()
        gcopies.append(g)
    lcopy = pltpu.make_async_copy(leaf, lbuf, lsem.at[9])
    lcopy.start()
    bcopies = []
    for i in range(4):
        b = pltpu.make_async_copy(
            bins.at[pl.ds(i * quarter, quarter), pl.ds(pl.multiple_of((o // 2) * 128, 128), 128)],
            bbuf.at[pl.ds(i * quarter, quarter), :],
            lsem.at[4 + i],
        )
        b.start()
        bcopies.append(b)

    def row_id(xx, zz, yy):
        return xx * (NZ * NY) + zz * NY + yy

    def target(delta):
        return row_id((x + delta // NZ) % NX, (z + delta % NZ) % NZ, y)

    here = row_id(x, z, y)
    barrier = pltpu.get_barrier_semaphore()
    for d in range(1, NO):
        pl.semaphore_signal(barrier, inc=1, device_id=(here, (o + d) % NO), device_id_type=MESH)
    for d in range(1, NY):
        pl.semaphore_signal(barrier, inc=1, device_id=(row_id(x, z, (y + d) % NY), o), device_id_type=MESH)

    def greet(delta, carry):
        pl.semaphore_signal(barrier, inc=1, device_id=(target(delta), o), device_id_type=MESH)
        return carry

    lax.fori_loop(1, STEPS, greet, 0)

    pcopy.wait()
    pmat = pbuf[pl.ds(pl.multiple_of(o * 256, 256), 256), :]

    def quarter_copy(i, d):
        return pltpu.make_async_remote_copy(
            src_ref=part.at[i], dst_ref=skin.at[d - 1], send_sem=qs_send.at[d - 1], recv_sem=qs_recv.at[d - 1],
            device_id=(here, (o + d) % NO), device_id_type=MESH,
        )

    for i, d in enumerate(order):
        gcopies[i].wait()
        part[i] = lax.dot_general(pmat, gbuf[i], (((0,), (1,)), ((), ())), preferred_element_type=F32)
        if i == 0:
            pl.semaphore_wait(barrier, (NO - 1) + (NY - 1) + (STEPS - 1))
        if d:
            quarter_copy(i, d).start()

    lcopy.wait()
    own_col = lax.broadcasted_iota(jnp.int32, (64, 128), 1) - (o % 2) * 64
    pick = (own_col == lax.broadcasted_iota(jnp.int32, (64, 128), 0)).astype(F32).astype(BF)

    def turn(i):
        bcopies[i].wait()
        block = bbuf[pl.ds(i * quarter, quarter), :].astype(F32).astype(BF)
        b = lax.dot_general(pick, block, (((1,), (1,)), ((), ())), preferred_element_type=F32)
        high = jnp.floor(b * F32(1.0 / 16.0))
        low = b - high * F32(16.0)
        lanes = pl.ds(i * quarter, quarter)
        bh[:, lanes] = high
        tiles = quarter // 128
        for t in range(tiles):
            leaf_row = lbuf[pl.ds(i * tiles + t, 1), :].astype(F32) * F32(16.0)
            cc[:, pl.ds(i * quarter + t * 128, 128)] = low[:, t * 128:(t + 1) * 128] + leaf_row

    turn(0)
    turn(1)
    for d in range(1, NO):
        quarter_copy(0, d).wait_recv()
    mine = ((part[3] + skin[0]) + (skin[1] + skin[2]))
    skq[...] = jnp.concatenate([mine[:, :half], mine[:, half:]], 0).astype(BF)

    def gather_copy(d):
        return pltpu.make_async_remote_copy(
            src_ref=skq, dst_ref=skr.at[d - 1], send_sem=ag_send.at[d - 1], recv_sem=ag_recv.at[d - 1],
            device_id=(here, (o + d) % NO), device_id_type=MESH,
        )

    for d in (2, 1, 3):
        gather_copy(d).start()
    turn(2)
    turn(3)

    def spread(packed, owner):
        wide = packed.astype(F32)
        for h in range(2):
            rows8 = wide[8 * h:8 * h + 8]
            sk16[:, pl.ds(pl.multiple_of(owner * quarter + h * half, half), half)] = jnp.concatenate(
                [rows8, rows8], 0
            ).astype(BF)

    spread(skq[...], o)
    for d in range(1, NO):
        gather_copy(d).wait_recv()
        spread(skr[d - 1], (o + NO - d) % NO)

    sub16 = lax.broadcasted_iota(jnp.int32, (16, rows), 0)
    pair = (sub16 // 8).astype(F32).astype(BF)
    sixteen = sub16.astype(F32).astype(BF)
    lane = lax.broadcasted_iota(jnp.int32, (32, 128), 1)

    def y_copy(t, d):
        to = (y + d) % NY
        return pltpu.make_async_remote_copy(
            src_ref=sbuf.at[t, to], dst_ref=rbuf1.at[t, d - 1], send_sem=y_send.at[t, d - 1],
            recv_sem=y_recv.at[t, d - 1], device_id=(row_id(x, z, to), o), device_id_type=MESH,
        )

    def z_copy(t):
        return pltpu.make_async_remote_copy(
            src_ref=s2.at[t], dst_ref=rbuf2.at[t], send_sem=z_send.at[t], recv_sem=z_recv.at[t],
            device_id=(target(STEPS - 1 - t), o), device_id_type=MESH,
        )

    def gather_y(t):
        for d in range(1, NY):
            y_copy(t, d).wait_recv()
        return (fbuf[t, y] + rbuf1[t, 0].astype(F32)) + (rbuf1[t, 1].astype(F32) + rbuf1[t, 2].astype(F32))

    def send_on(t):
        s2[t] = gather_y(t)
        z_copy(t).start()

    def step(t, carry):
        delta = STEPS - 1 - t
        base = (((x + delta // NZ) % NX) * NZ + (z + delta % NZ) % NZ) * NY
        weights = sk16[...]
        left, right = [], []
        for f in range(NY):
            b16 = jnp.broadcast_to(bh[pl.ds(base + f, 1), :], (16, rows)).astype(BF)
            c16 = jnp.broadcast_to(cc[pl.ds(base + f, 1), :], (16, rows)).astype(BF)
            for m in range(4):
                left.append(jnp.where(b16 == pair + BF(2 * m), weights, BF(0)))
            for m in range(4):
                right.append(jnp.where(c16 == sixteen + BF(16 * m), BF(1), BF(0)))
        both = lax.dot_general(
            jnp.concatenate(left, 0), jnp.concatenate(right, 0), (((1,), (1,)), ((), ())),
            preferred_element_type=F32,
        )
        for f in range(NY):
            block = both[f * 64:(f + 1) * 64, (f // 2) * 128:(f // 2) * 128 + 128]
            turned = pltpu.roll(block, 64, 1)
            low, high = (block, turned) if f % 2 == 0 else (turned, block)
            folded = jnp.where(lane < 64, low[:32], high[32:])
            fbuf[t, f] = folded
            sbuf[t, f] = folded.astype(BF)
        for d in (2, 1, 3):
            y_copy(t, d).start()

        @pl.when(t >= LAG)
        def _():
            send_on(t - LAG)

        return carry

    lax.fori_loop(0, STEPS, step, 0)
    for t in range(STEPS - LAG, STEPS - 1):
        send_on(t)
    total = gather_y(STEPS - 1)

    def add(t, acc):
        z_copy(t).wait_recv()
        return acc + rbuf2[t]

    total = lax.fori_loop(0, STEPS - 1, add, total) * F32(scale)
    seg = (lax.broadcasted_iota(jnp.int32, (8, 128), 1) // 16) % 4
    for l in range(LEAVES):
        res = jnp.zeros((8, 128), F32)
        for q in range(4):
            moved = total[8 * q:8 * q + 8]
            shift = ((q - l) * 16) % 128
            if shift:
                moved = pltpu.roll(moved, shift, 1)
            res = jnp.where(seg == q, moved, res)
        out[l] = res

    for i, d in enumerate(order):
        if d:
            quarter_copy(i, d).wait_send()
            gather_copy(d).wait_send()

    def drain(t, carry):
        for d in range(1, NY):
            y_copy(t, d).wait_send()

        @pl.when(t < STEPS - 1)
        def _():
            z_copy(t).wait_send()

        return carry

    lax.fori_loop(0, STEPS, drain, 0)


def local(scale, grads, projection, bins, leaf):
    rows = grads.shape[0]
    quarter = rows // NO
    any_spec = pl.BlockSpec(memory_space=pl.ANY)
    dma = pltpu.SemaphoreType.DMA
    result = pl.pallas_call(
        functools.partial(kernel, scale),
        out_shape=jax.ShapeDtypeStruct((LEAVES, SK, BINS), F32),
        in_specs=[any_spec] * 4,
        out_specs=pl.BlockSpec(memory_space=pltpu.VMEM),
        scratch_shapes=[
            pltpu.VMEM((NO, quarter, grads.shape[1]), BF),
            pltpu.VMEM(projection.shape, BF),
            pltpu.VMEM((rows, 128), jnp.int32),
            pltpu.VMEM((rows // 128, 128), jnp.int32),
            pltpu.VMEM((NO, SK, quarter), F32),
            pltpu.VMEM((NO - 1, SK, quarter), F32),
            pltpu.VMEM((2 * SK, quarter // 2), BF),
            pltpu.VMEM((NO - 1, 2 * SK, quarter // 2), BF),
            pltpu.VMEM((2 * SK, rows), BF),
            pltpu.VMEM((64, rows), F32),
            pltpu.VMEM((64, rows), F32),
            pltpu.VMEM((STEPS, NY, 32, 128), F32),
            pltpu.VMEM((STEPS, NY, 32, 128), BF),
            pltpu.VMEM((STEPS, NY - 1, 32, 128), BF),
            pltpu.VMEM((STEPS - 1, 32, 128), F32),
            pltpu.VMEM((STEPS - 1, 32, 128), F32),
            dma((10,)), dma,
            dma((NO - 1,)), dma((NO - 1,)), dma((NO - 1,)), dma((NO - 1,)),
            dma((STEPS, NY - 1)), dma((STEPS, NY - 1)), dma((STEPS - 1,)), dma((STEPS - 1,)),
        ],
        compiler_params=pltpu.CompilerParams(
            collective_id=0, has_side_effects=True, vmem_limit_bytes=60 << 20
        ),
        name="sketch_histogram",
    )(grads, projection, bins, leaf.reshape(rows // 128, 128))
    return result.reshape(1, 1, LEAVES, SK, BINS)


def solution(mesh):
    placed = (P("rows", "outs"), P(), P("rows", None), P("rows"))

    def whole(grads, projection, bins, leaf):
        scale = math.sqrt(LEAVES * BINS / grads.shape[0])
        return jax.shard_map(
            functools.partial(local, scale),
            mesh=mesh,
            in_specs=placed,
            out_specs=P("rows", "outs", None, None, None),
            check_vma=False,
        )(grads, projection, bins, leaf)

    return whole
```

time: 1500 us -> 49.5 us (0.03)
  the two profiles are of different devices: /device:TPU:0 before, /device:TPU:32 now
where the time goes in v1:
time: 49.5 us; the launch traced here: 49.2 us
  Pallas kernels  46.4 us (94%)
  local copies, waits for them, and re-layouts  2.87 us (6%)
    pallas_call x1, Pallas kernels, local(): pl.pallas_call(functools.partial(kernel, scale), out_shape=jax.ShapeDtype...  46.4 us
    unnamed x2, local copies, waits for them, and re-layouts  2.87 us

profile of v1, /device:TPU:32, one launch (start us, length us, event | category | flops | bytes accessed | tf_op | source)
XLA Modules:
  0.0 49.2 jit_solution(11372190413039143241)
XLA Ops:
  0.0 1.5 %copy.5.proj = bf16[1024,8]{1,0:T(8,128)(2,1)} copy(bf16[1024,8]{0,1:T(8,128)(2,1)} %param.5) | data formatting | bytes 32768 | tf_op args[1]
  1.5 46.4 %sketch_histogram.1 = f32[4,8,128]{2,1,0:T(8,128)} custom-call(bf16[6144,256]{1,0:T(8,128)(2,1)} %grads.1, bf16[1024,8]{1,0:T(8,128)(2,1)} %copy.5.proj, s32[6144,256]{1,0:T(8,128)} %bins.1, s32[48,128]{1,0:T(8,128)} %bitcast.3), custom_call_target="tpu_custom_call" | custom-call | tf_op jit(solution)/shard_map/sketch_histogram/pallas_call | solution.py:251
  47.9 1.3 %copy.7 = f32[1,1,4,8,128]{4,3,2,1,0:T(8,128)} copy(f32[1,1,4,8,128]{4,3,2,1,0:T(8,128)} %bitcast.2) | data formatting | bytes 32768

commit v2 on v1

--- a/solution.py
+++ b/solution.py
@@ -16,7 +16,9 @@
 F32 = jnp.float32
 NX, NZ, NY, NO = 2, 8, 4, 4
 STEPS = NX * NZ
-LAG = 2
+PAIRS = STEPS // NX
+OPEN = 2
+LAG = 3
 
 
 def pieces(n_rows):
@@ -30,7 +32,7 @@
     out,
     gbuf, pbuf, bbuf, lbuf, part, skin, skq, skr, sk16, bh, cc,
     fbuf, sbuf, rbuf1, s2, rbuf2,
-    lsem, osem, qs_send, qs_recv, ag_send, ag_recv, y_send, y_recv, z_send, z_recv,
+    lsem, ready, go, qs_send, qs_recv, ag_send, ag_recv, y_send, y_recv, z_send, z_recv,
 ):
     x, z, y = pieces(NX * NZ * NY)
     o = lax.axis_index("outs")
@@ -58,30 +60,24 @@
             bbuf.at[pl.ds(i * quarter, quarter), :],
             lsem.at[4 + i],
         )
-        b.start()
         bcopies.append(b)
 
     def row_id(xx, zz, yy):
         return xx * (NZ * NY) + zz * NY + yy
 
-    def target(delta):
-        return row_id((x + delta // NZ) % NX, (z + delta % NZ) % NZ, y)
+    def group(t):
+        return (x + 1 - t % 2) % NX, (z + 1 + t // 2) % NZ
 
     here = row_id(x, z, y)
     barrier = pltpu.get_barrier_semaphore()
+    leads = o == 0
     for d in range(1, NO):
-        pl.semaphore_signal(barrier, inc=1, device_id=(here, (o + d) % NO), device_id_type=MESH)
-    for d in range(1, NY):
-        pl.semaphore_signal(barrier, inc=1, device_id=(row_id(x, z, (y + d) % NY), o), device_id_type=MESH)
-
-    def greet(delta, carry):
-        pl.semaphore_signal(barrier, inc=1, device_id=(target(delta), o), device_id_type=MESH)
-        return carry
-
-    lax.fori_loop(1, STEPS, greet, 0)
+        @pl.when((o + d) % NO != 0)
+        def _(d=d):
+            pl.semaphore_signal(barrier, inc=1, device_id=(here, (o + d) % NO), device_id_type=MESH)
 
     pcopy.wait()
-    pmat = pbuf[pl.ds(pl.multiple_of(o * 256, 256), 256), :]
+    pmat = pbuf[:, pl.ds(pl.multiple_of(o * 256, 256), 256)]
 
     def quarter_copy(i, d):
         return pltpu.make_async_remote_copy(
@@ -91,9 +87,30 @@
 
     for i, d in enumerate(order):
         gcopies[i].wait()
-        part[i] = lax.dot_general(pmat, gbuf[i], (((0,), (1,)), ((), ())), preferred_element_type=F32)
+        if i == 1:
+            for b in bcopies:
+                b.start()
+        part[i] = lax.dot_general(pmat, gbuf[i], (((1,), (1,)), ((), ())), preferred_element_type=F32)
         if i == 0:
-            pl.semaphore_wait(barrier, (NO - 1) + (NY - 1) + (STEPS - 1))
+            @pl.when(jnp.logical_not(leads))
+            def _():
+                pl.semaphore_wait(barrier, NO - 1)
+                pl.semaphore_signal(ready, inc=1, device_id=(here, 0), device_id_type=MESH)
+
+            @pl.when(leads)
+            def _():
+                pl.semaphore_wait(ready, NO - 1)
+                for d in range(1, NY):
+                    pl.semaphore_signal(
+                        barrier, inc=1, device_id=(row_id(x, z, (y + d) % NY), 0), device_id_type=MESH
+                    )
+
+                def greet(t, carry):
+                    pl.semaphore_signal(barrier, inc=1, device_id=(row_id(*group(t), y), 0), device_id_type=MESH)
+                    return carry
+
+                lax.fori_loop(0, STEPS - 1, greet, 0)
+
         if d:
             quarter_copy(i, d).start()
 
@@ -150,31 +167,38 @@
     sixteen = sub16.astype(F32).astype(BF)
     lane = lax.broadcasted_iota(jnp.int32, (32, 128), 1)
 
-    def y_copy(t, d):
+    def y_copy(i, d):
         to = (y + d) % NY
         return pltpu.make_async_remote_copy(
-            src_ref=sbuf.at[t, to], dst_ref=rbuf1.at[t, d - 1], send_sem=y_send.at[t, d - 1],
-            recv_sem=y_recv.at[t, d - 1], device_id=(row_id(x, z, to), o), device_id_type=MESH,
+            src_ref=sbuf.at[i, to], dst_ref=rbuf1.at[i, d - 1], send_sem=y_send.at[i, d - 1],
+            recv_sem=y_recv.at[i, d - 1], device_id=(row_id(x, z, to), o), device_id_type=MESH,
         )
 
     def z_copy(t):
         return pltpu.make_async_remote_copy(
             src_ref=s2.at[t], dst_ref=rbuf2.at[t], send_sem=z_send.at[t], recv_sem=z_recv.at[t],
-            device_id=(target(STEPS - 1 - t), o), device_id_type=MESH,
-        )
-
-    def gather_y(t):
+            device_id=(row_id(*group(t), y), o), device_id_type=MESH,
+        )
+
+    def send_y(i):
+        for d in (2, 1, 3):
+            y_copy(i, d).start()
+
+    def gather_y(i):
         for d in range(1, NY):
-            y_copy(t, d).wait_recv()
-        return (fbuf[t, y] + rbuf1[t, 0].astype(F32)) + (rbuf1[t, 1].astype(F32) + rbuf1[t, 2].astype(F32))
-
-    def send_on(t):
-        s2[t] = gather_y(t)
-        z_copy(t).start()
-
-    def step(t, carry):
-        delta = STEPS - 1 - t
-        base = (((x + delta // NZ) % NX) * NZ + (z + delta % NZ) % NZ) * NY
+            y_copy(i, d).wait_recv()
+        return [
+            (fbuf[i, y, u] + rbuf1[i, 0, u].astype(F32)) + (rbuf1[i, 1, u].astype(F32) + rbuf1[i, 2, u].astype(F32))
+            for u in range(NX)
+        ]
+
+    def send_on(i):
+        for u, block in enumerate(gather_y(i)):
+            s2[NX * i + u] = block
+            z_copy(NX * i + u).start()
+
+    def histogram(i, u):
+        base = row_id(*group(NX * i + u), 0)
         weights = sk16[...]
         left, right = [], []
         for f in range(NY):
@@ -193,21 +217,44 @@
             turned = pltpu.roll(block, 64, 1)
             low, high = (block, turned) if f % 2 == 0 else (turned, block)
             folded = jnp.where(lane < 64, low[:32], high[32:])
-            fbuf[t, f] = folded
-            sbuf[t, f] = folded.astype(BF)
-        for d in (2, 1, 3):
-            y_copy(t, d).start()
-
-        @pl.when(t >= LAG)
+            fbuf[i, f, u] = folded
+            sbuf[i, f, u] = folded.astype(BF)
+
+    def step(i, carry):
+        for u in range(NX):
+            histogram(i, u)
+
+        @pl.when(i == OPEN)
         def _():
-            send_on(t - LAG)
+            @pl.when(leads)
+            def _():
+                pl.semaphore_wait(barrier, (NY - 1) + (STEPS - 1))
+                for d in range(1, NO):
+                    pl.semaphore_signal(go, inc=1, device_id=(here, d), device_id_type=MESH)
+
+            @pl.when(jnp.logical_not(leads))
+            def _():
+                pl.semaphore_wait(go, 1)
+
+            for early in range(OPEN):
+                send_y(early)
+
+        @pl.when(i >= OPEN)
+        def _():
+            send_y(i)
+
+        @pl.when(i >= LAG)
+        def _():
+            send_on(i - LAG)
 
         return carry
 
-    lax.fori_loop(0, STEPS, step, 0)
-    for t in range(STEPS - LAG, STEPS - 1):
-        send_on(t)
-    total = gather_y(STEPS - 1)
+    lax.fori_loop(0, PAIRS, step, 0)
+    for i in range(PAIRS - LAG, PAIRS - 1):
+        send_on(i)
+    other, total = gather_y(PAIRS - 1)
+    s2[STEPS - 2] = other
+    z_copy(STEPS - 2).start()
 
     def add(t, acc):
         z_copy(t).wait_recv()
@@ -230,17 +277,17 @@
             quarter_copy(i, d).wait_send()
             gather_copy(d).wait_send()
 
-    def drain(t, carry):
+    def drain_y(i, carry):
         for d in range(1, NY):
-            y_copy(t, d).wait_send()
-
-        @pl.when(t < STEPS - 1)
-        def _():
-            z_copy(t).wait_send()
-
+            y_copy(i, d).wait_send()
         return carry
 
-    lax.fori_loop(0, STEPS, drain, 0)
+    def drain_z(t, carry):
+        z_copy(t).wait_send()
+        return carry
+
+    lax.fori_loop(0, PAIRS, drain_y, 0)
+    lax.fori_loop(0, STEPS - 1, drain_z, 0)
 
 
 def local(scale, grads, projection, bins, leaf):
@@ -255,7 +302,7 @@
         out_specs=pl.BlockSpec(memory_space=pltpu.VMEM),
         scratch_shapes=[
             pltpu.VMEM((NO, quarter, grads.shape[1]), BF),
-            pltpu.VMEM(projection.shape, BF),
+            pltpu.VMEM(projection.shape[::-1], BF),
             pltpu.VMEM((rows, 128), jnp.int32),
             pltpu.VMEM((rows // 128, 128), jnp.int32),
             pltpu.VMEM((NO, SK, quarter), F32),
@@ -265,20 +312,20 @@
             pltpu.VMEM((2 * SK, rows), BF),
             pltpu.VMEM((64, rows), F32),
             pltpu.VMEM((64, rows), F32),
-            pltpu.VMEM((STEPS, NY, 32, 128), F32),
-            pltpu.VMEM((STEPS, NY, 32, 128), BF),
-            pltpu.VMEM((STEPS, NY - 1, 32, 128), BF),
+            pltpu.VMEM((PAIRS, NY, NX, 32, 128), F32),
+            pltpu.VMEM((PAIRS, NY, NX, 32, 128), BF),
+            pltpu.VMEM((PAIRS, NY - 1, NX, 32, 128), BF),
             pltpu.VMEM((STEPS - 1, 32, 128), F32),
             pltpu.VMEM((STEPS - 1, 32, 128), F32),
-            dma((10,)), dma,
+            dma((10,)), pltpu.SemaphoreType.REGULAR, pltpu.SemaphoreType.REGULAR,
             dma((NO - 1,)), dma((NO - 1,)), dma((NO - 1,)), dma((NO - 1,)),
-            dma((STEPS, NY - 1)), dma((STEPS, NY - 1)), dma((STEPS - 1,)), dma((STEPS - 1,)),
+            dma((PAIRS, NY - 1)), dma((PAIRS, NY - 1)), dma((STEPS - 1,)), dma((STEPS - 1,)),
         ],
         compiler_params=pltpu.CompilerParams(
             collective_id=0, has_side_effects=True, vmem_limit_bytes=60 << 20
         ),
         name="sketch_histogram",
-    )(grads, projection, bins, leaf.reshape(rows // 128, 128))
+    )(grads, projection.T, bins, leaf.reshape(rows // 128, 128))
     return result.reshape(1, 1, LEAVES, SK, BINS)
 
 

time: 49.5 us -> 42.2 us (0.85)
  Pallas kernels: 46.4 us -> 40.5 us
  local copies, waits for them, and re-layouts: 2.87 us -> 1.32 us
    pallas_call x1, Pallas kernels: 46.4 us -> 40.5 us  [local(): pl.pallas_call(functools.partial(kernel, scale), out_shape=jax.ShapeDtype...]
    unnamed x2 -> x1, local copies, waits for them, and re-layouts: 2.87 us -> 1.32 us
where the time goes in v2:
time: 42.2 us; the launch traced here: 41.8 us
  Pallas kernels  40.5 us (96%)
  local copies, waits for them, and re-layouts  1.32 us (3%)
    pallas_call x1, Pallas kernels, local(): pl.pallas_call(functools.partial(kernel, scale), out_shape=jax.ShapeDtype...  40.5 us
    unnamed x1, local copies, waits for them, and re-layouts  1.32 us

profile of v2, /device:TPU:32, one launch (start us, length us, event | category | flops | bytes accessed | tf_op | source)
XLA Modules:
  0.0 41.8 jit_solution(985603115956417829)
XLA Ops:
  0.0 40.5 %sketch_histogram.1 = f32[4,8,128]{2,1,0:T(8,128)} custom-call(bf16[6144,256]{1,0:T(8,128)(2,1)} %grads.1, bf16[8,1024]{1,0:T(8,128)(2,1)} %bitcast.5, s32[6144,256]{1,0:T(8,128)} %bins.1, s32[48,128]{1,0:T(8,128)} %bitcast.4), custom_call_target="tpu_custom_call" | custom-call | tf_op jit(solution)/shard_map/sketch_histogram/pallas_call | solution.py:298
  40.5 1.3 %copy.6 = f32[1,1,4,8,128]{4,3,2,1,0:T(8,128)} copy(f32[1,1,4,8,128]{4,3,2,1,0:T(8,128)} %bitcast.3) | data formatting | bytes 32768

commit v3 on v2

v3 whole, which is shorter than its diff:
```python
import functools
import math

import jax
import jax.numpy as jnp
from jax import lax
from jax.experimental import pallas as pl
from jax.experimental.pallas import tpu as pltpu
from jax.sharding import PartitionSpec as P

SK = 8
BINS = 128
LEAVES = 4
MESH = pl.DeviceIdType.MESH
BF = jnp.bfloat16
F32 = jnp.float32
NX, NZ, NY, NO = 2, 8, 4, 4
STEPS = NX * NZ
ROUNDS = STEPS // NX
BATCHES = ((0, 4), (4, 4), (8, 4), (12, 2), (14, 2))
DEPTH = 256


def pieces(n_rows):
    r = lax.axis_index("rows")
    return r // (NZ * NY), (r // NY) % NZ, r % NY


def kernel(
    scale,
    grads, proj, bins, leaf,
    out,
    gbuf, pbuf, bbuf, lbuf, part, skin, skq, skr, sk16, bh, cc,
    fbuf, sbuf, rbuf1, s2, rbuf2,
    lsem, ready, go, qs_send, qs_recv, ag_send, ag_recv, y_send, y_recv, z_send, z_recv,
):
    x, z, y = pieces(NX * NZ * NY)
    o = lax.axis_index("outs")
    rows = bh.shape[1]
    quarter = rows // NO
    half = quarter // 2
    order = (2, 1, 3, 0)

    pcopy = pltpu.make_async_copy(proj, pbuf, lsem.at[8])
    pcopy.start()
    gcopies = []
    for i, d in enumerate(order):
        q = (o + d) % NO
        g = pltpu.make_async_copy(
            grads.at[pl.ds(pl.multiple_of(q * quarter, quarter), quarter), :], gbuf.at[i], lsem.at[i]
        )
        g.start()
        gcopies.append(g)
    lcopy = pltpu.make_async_copy(leaf, lbuf, lsem.at[9])
    lcopy.start()
    bcopies = []
    for i in range(4):
        b = pltpu.make_async_copy(
            bins.at[pl.ds(i * quarter, quarter), pl.ds(pl.multiple_of((o // 2) * 128, 128), 128)],
            bbuf.at[pl.ds(i * quarter, quarter), :],
            lsem.at[4 + i],
        )
        bcopies.append(b)

    def row_id(xx, zz, yy):
        return xx * (NZ * NY) + zz * NY + yy

    def group(t):
        w = t - 7 * (t // 8)
        return (x + w + (w % 8) // 6) % NX, ((z // 4 + 1 - t // 8) % 2) * 4 + (z % 4 + w // 2) % 4

    here = row_id(x, z, y)
    barrier = pltpu.get_barrier_semaphore()
    leads = o == 0
    for d in range(1, NO):
        @pl.when((o + d) % NO != 0)
        def _(d=d):
            pl.semaphore_signal(barrier, inc=1, device_id=(here, (o + d) % NO), device_id_type=MESH)

    pcopy.wait()
    wide = pbuf[:, pl.ds(pl.multiple_of(o * 256, 256), 256)].astype(F32)
    pmat = jnp.concatenate([wide, wide], 0).astype(BF)

    def multiply(left, rights, take):
        def body(*accs):
            for n, right in enumerate(rights):
                pltpu.matmul_push_rhs(right, (n // 2) % 2, n % 2, transpose=True)
                pltpu.matmul_acc_lhs(accs[n], left, load_staged_rhs=(n // 2) % 2)
            for n in range(len(rights)):
                take(n, pltpu.matmul_pop(accs[n]))

        pl.run_scoped(body, *(pltpu.ACC(n % 2)((left.shape[0], DEPTH), F32) for n in range(len(rights))))

    def put_part(i, n, value):
        part[i, :, pl.ds(n * DEPTH, DEPTH)] = value[:SK]

    def quarter_copy(i, d):
        return pltpu.make_async_remote_copy(
            src_ref=part.at[i], dst_ref=skin.at[d - 1], send_sem=qs_send, recv_sem=qs_recv,
            device_id=(here, (o + d) % NO), device_id_type=MESH,
        )

    def enter():
        @pl.when(jnp.logical_not(leads))
        def _():
            pl.semaphore_wait(barrier, NO - 1)
            pl.semaphore_signal(ready, inc=1, device_id=(here, 0), device_id_type=MESH)

        @pl.when(leads)
        def _():
            pl.semaphore_wait(ready, NO - 1)

    for i, d in enumerate(order):
        gcopies[i].wait()
        if i == 1:
            for b in bcopies:
                b.start()
        multiply(
            pmat, [gbuf[i, pl.ds(n * DEPTH, DEPTH), :] for n in range(quarter // DEPTH)],
            lambda n, value: put_part(i, n, value),
        )
        if i == 0:
            enter()
        if d:
            quarter_copy(i, d).start()

    @pl.when(leads)
    def _():
        for d in range(1, NY):
            pl.semaphore_signal(
                barrier, inc=1, device_id=(row_id(x, z, (y + d) % NY), 0), device_id_type=MESH
            )

        def greet(t, carry):
            pl.semaphore_signal(barrier, inc=1, device_id=(row_id(*group(t), y), 0), device_id_type=MESH)
            return carry

        lax.fori_loop(0, STEPS - 1, greet, 0)

    lcopy.wait()
    row_at = lax.broadcasted_iota(jnp.int32, (128, 256), 0)
    col_at = lax.broadcasted_iota(jnp.int32, (128, 256), 1)
    wanted = (row_at // 64) * 128 + (o % 2) * 64 + row_at % 64
    pick = (col_at == wanted).astype(F32).astype(BF)
    per_row = 128

    def put_bins(i, n, value):
        for h in range(2):
            b = value[64 * h:64 * h + 64]
            high = jnp.floor(b * F32(1.0 / 16.0))
            low = b - high * F32(16.0)
            at = i * quarter + (2 * n + h) * DEPTH
            bh[:, pl.ds(at, DEPTH)] = high
            for t in range(DEPTH // per_row):
                leaf_row = lbuf[pl.ds(at // per_row + t, 1), :].astype(F32) * F32(16.0)
                cc[:, pl.ds(at + t * per_row, per_row)] = low[:, t * per_row:(t + 1) * per_row] + leaf_row

    def turn(i):
        bcopies[i].wait()
        blocks = [
            bbuf[pl.ds(i * quarter + n * DEPTH, DEPTH), :].astype(F32).astype(BF) for n in range(quarter // DEPTH)
        ]
        multiply(
            pick, [jnp.concatenate(blocks[n:n + 2], 1) for n in range(0, len(blocks), 2)],
            lambda n, value: put_bins(i, n, value),
        )

    turn(0)
    turn(1)
    pltpu.make_async_copy(skin, skin, qs_recv).wait()
    mine = ((part[3] + skin[0]) + (skin[1] + skin[2]))
    skq[...] = jnp.concatenate([mine[:, :half], mine[:, half:]], 0).astype(BF)

    def gather_copy(d):
        return pltpu.make_async_remote_copy(
            src_ref=skq, dst_ref=skr.at[d - 1], send_sem=ag_send, recv_sem=ag_recv,
            device_id=(here, (o + d) % NO), device_id_type=MESH,
        )

    for d in (2, 1, 3):
        gather_copy(d).start()
    turn(2)
    turn(3)

    def spread(packed, owner):
        wide = packed.astype(F32)
        for h in range(2):
            rows8 = wide[8 * h:8 * h + 8]
            sk16[:, pl.ds(pl.multiple_of(owner * quarter + h * half, half), half)] = jnp.concatenate(
                [rows8, rows8], 0
            ).astype(BF)

    spread(skq[...], o)
    pltpu.make_async_copy(skr, skr, ag_recv).wait()
    for d in range(1, NO):
        spread(skr[d - 1], (o + NO - d) % NO)

    sub16 = lax.broadcasted_iota(jnp.int32, (16, DEPTH), 0)
    pair = (sub16 // 8).astype(F32).astype(BF)
    sixteen = sub16.astype(F32).astype(BF)
    lane = lax.broadcasted_iota(jnp.int32, (32, 128), 1)

    def y_copy(b, d):
        to, (first, n) = (y + d) % NY, BATCHES[b]
        return pltpu.make_async_remote_copy(
            src_ref=sbuf.at[to, pl.ds(first, n)], dst_ref=rbuf1.at[d - 1, pl.ds(first, n)], send_sem=y_send,
            recv_sem=y_recv.at[b], device_id=(row_id(x, z, to), o), device_id_type=MESH,
        )

    def z_copy(t):
        return pltpu.make_async_remote_copy(
            src_ref=s2.at[t], dst_ref=rbuf2.at[t], send_sem=z_send, recv_sem=z_recv,
            device_id=(row_id(*group(t), y), o), device_id_type=MESH,
        )

    def send_y(b):
        for d in (2, 1, 3):
            y_copy(b, d).start()

    def gather_y(b):
        first, n = BATCHES[b]
        came = rbuf1.at[:, pl.ds(first, n)]
        pltpu.make_async_copy(came, came, y_recv.at[b]).wait()
        return [
            (fbuf[y, t] + rbuf1[0, t].astype(F32)) + (rbuf1[1, t].astype(F32) + rbuf1[2, t].astype(F32))
            for t in range(first, first + n)
        ]

    def send_on(b):
        for t, block in enumerate(gather_y(b), BATCHES[b][0]):
            s2[t] = block
            z_copy(t).start()

    def feed(acc, unit, base, k, slot):
        lanes = pl.ds(k * DEPTH, DEPTH)
        weights = sk16[:, lanes]
        left, right = [], []
        for f in range(NY):
            b16 = jnp.broadcast_to(bh[pl.ds(base + f, 1), lanes], (16, DEPTH)).astype(BF)
            c16 = jnp.broadcast_to(cc[pl.ds(base + f, 1), lanes], (16, DEPTH)).astype(BF)
            for m in range(4):
                left.append(jnp.where(b16 == pair + BF(2 * m), weights, BF(0)))
                right.append(jnp.where(c16 == sixteen + BF(16 * m), BF(1), BF(0)))
        pltpu.matmul_push_rhs(jnp.concatenate(right, 0), slot, unit, transpose=True)
        pltpu.matmul_acc_lhs(acc, jnp.concatenate(left, 0), load_staged_rhs=slot)

    def keep(t, both):
        for f in range(NY):
            block = both[f * 64:(f + 1) * 64, (f // 2) * 128:(f // 2) * 128 + 128]
            turned = pltpu.roll(block, 64, 1)
            low, high = (block, turned) if f % 2 == 0 else (turned, block)
            folded = jnp.where(lane < 64, low[:32], high[32:])
            fbuf[f, t] = folded
            sbuf[f, t] = folded.astype(BF)

    def with_sums(body):
        pl.run_scoped(body, *(pltpu.ACC(unit)((256, 256), F32) for unit in range(2)))

    def two_groups(i):
        bases = [row_id(*group(NX * i + u), 0) for u in range(NX)]

        def body(*sums):
            for k in range(rows // DEPTH):
                for u in range(NX):
                    feed(sums[u], u, bases[u], k, k % 2)
            for u in range(NX):
                keep(NX * i + u, pltpu.matmul_pop(sums[u]))

        with_sums(body)

    late = z // (NZ // 2) == 1

    def open_sends():
        @pl.when(leads)
        def _():
            pl.semaphore_wait(barrier, (NY - 1) + (STEPS - 1))
            for d in range(1, NO):
                pl.semaphore_signal(go, inc=1, device_id=(here, d), device_id_type=MESH)

        @pl.when(jnp.logical_not(leads))
        def _():
            pl.semaphore_wait(go, 1)

        send_y(0)

    def step(i, carry):
        two_groups(i)

        @pl.when(jnp.logical_and(i == 1, late))
        def _():
            open_sends()

        @pl.when(i == 3)
        def _():
            @pl.when(jnp.logical_not(late))
            def _():
                open_sends()

            send_y(1)

            @pl.when(late)
            def _():
                send_on(0)

        @pl.when(i == 5)
        def _():
            send_y(2)

            @pl.when(jnp.logical_not(late))
            def _():
                send_on(0)

            send_on(1)

        @pl.when(i == 6)
        def _():
            send_y(3)
            send_on(2)

        return carry

    lax.fori_loop(0, ROUNDS, step, 0)
    send_y(4)
    send_on(3)
    near, total = gather_y(4)
    s2[STEPS - 2] = near
    z_copy(STEPS - 2).start()
    pltpu.make_async_copy(rbuf2, rbuf2, z_recv).wait()
    for t in range(STEPS - 1):
        total = total + rbuf2[t]
    total = total * F32(scale)
    seg = (lax.broadcasted_iota(jnp.int32, (8, 128), 1) // 16) % 4
    for l in range(LEAVES):
        res = jnp.zeros((8, 128), F32)
        for q in range(4):
            moved = total[8 * q:8 * q + 8]
            shift = ((q - l) * 16) % 128
            if shift:
                moved = pltpu.roll(moved, shift, 1)
            res = jnp.where(seg == q, moved, res)
        out[l] = res

    pltpu.make_async_copy(skin, skin, qs_send).wait()
    pltpu.make_async_copy(skr, skr, ag_send).wait()
    pltpu.make_async_copy(rbuf1, rbuf1, y_send).wait()
    pltpu.make_async_copy(rbuf2, rbuf2, z_send).wait()


def local(scale, grads, projection, bins, leaf):
    rows = grads.shape[0]
    quarter = rows // NO
    any_spec = pl.BlockSpec(memory_space=pl.ANY)
    dma = pltpu.SemaphoreType.DMA
    result = pl.pallas_call(
        functools.partial(kernel, scale),
        out_shape=jax.ShapeDtypeStruct((LEAVES, SK, BINS), F32),
        in_specs=[any_spec] * 4,
        out_specs=pl.BlockSpec(memory_space=pltpu.VMEM),
        scratch_shapes=[
            pltpu.VMEM((NO, quarter, grads.shape[1]), BF),
            pltpu.VMEM(projection.shape[::-1], BF),
            pltpu.VMEM((rows, 128), jnp.int32),
            pltpu.VMEM((rows // 128, 128), jnp.int32),
            pltpu.VMEM((NO, SK, quarter), F32),
            pltpu.VMEM((NO - 1, SK, quarter), F32),
            pltpu.VMEM((2 * SK, quarter // 2), BF),
            pltpu.VMEM((NO - 1, 2 * SK, quarter // 2), BF),
            pltpu.VMEM((2 * SK, rows), BF),
            pltpu.VMEM((64, rows), F32),
            pltpu.VMEM((64, rows), F32),
            pltpu.VMEM((NY, STEPS, 32, 128), F32),
            pltpu.VMEM((NY, STEPS, 32, 128), BF),
            pltpu.VMEM((NY - 1, STEPS, 32, 128), BF),
            pltpu.VMEM((STEPS - 1, 32, 128), F32),
            pltpu.VMEM((STEPS - 1, 32, 128), F32),
            dma((10,)), pltpu.SemaphoreType.REGULAR, pltpu.SemaphoreType.REGULAR,
            dma, dma, dma, dma, dma, dma((len(BATCHES),)), dma, dma,
        ],
        compiler_params=pltpu.CompilerParams(
            collective_id=0, has_side_effects=True, vmem_limit_bytes=54 << 20
        ),
        name="sketch_histogram",
    )(grads, projection.T, bins, leaf.reshape(rows // 128, 128))
    return result.reshape(1, 1, LEAVES, SK, BINS)


def solution(mesh):
    placed = (P("rows", "outs"), P(), P("rows", None), P("rows"))

    def whole(grads, projection, bins, leaf):
        scale = math.sqrt(LEAVES * BINS / grads.shape[0])
        return jax.shard_map(
            functools.partial(local, scale),
            mesh=mesh,
            in_specs=placed,
            out_specs=P("rows", "outs", None, None, None),
            check_vma=False,
        )(grads, projection, bins, leaf)

    return whole
```

time: 42.2 us -> 39.3 us (0.931)
  Pallas kernels: 40.5 us -> 37.7 us
    pallas_call x1, Pallas kernels: 40.5 us -> 37.7 us  [local(): pl.pallas_call(functools.partial(kernel, scale), out_shape=jax.ShapeDtype...]
where the time goes in v3:
time: 39.3 us; the launch traced here: 39 us
  Pallas kernels  37.7 us (96%)
  local copies, waits for them, and re-layouts  1.32 us (3%)
    pallas_call x1, Pallas kernels, local(): pl.pallas_call(functools.partial(kernel, scale), out_shape=jax.ShapeDtype...  37.7 us
    unnamed x1, local copies, waits for them, and re-layouts  1.32 us

profile of v3, /device:TPU:32, one launch (start us, length us, event | category | flops | bytes accessed | tf_op | source)
XLA Modules:
  0.0 39.0 jit_solution(8994589442716978585)
XLA Ops:
  0.0 37.7 %sketch_histogram.1 = f32[4,8,128]{2,1,0:T(8,128)} custom-call(bf16[6144,256]{1,0:T(8,128)(2,1)} %grads.1, bf16[8,1024]{1,0:T(8,128)(2,1)} %bitcast.5, s32[6144,256]{1,0:T(8,128)} %bins.1, s32[48,128]{1,0:T(8,128)} %bitcast.4), custom_call_target="tpu_custom_call" | custom-call | tf_op jit(solution)/shard_map/sketch_histogram/pallas_call | solution.py:354
  37.7 1.3 %copy.6 = f32[1,1,4,8,128]{4,3,2,1,0:T(8,128)} copy(f32[1,1,4,8,128]{4,3,2,1,0:T(8,128)} %bitcast.3) | data formatting | bytes 32768

commit v4 on v3

--- a/solution.py
+++ b/solution.py
@@ -377,7 +377,7 @@
             dma, dma, dma, dma, dma, dma((len(BATCHES),)), dma, dma,
         ],
         compiler_params=pltpu.CompilerParams(
-            collective_id=0, has_side_effects=True, vmem_limit_bytes=54 << 20
+            collective_id=0, has_side_effects=True, vmem_limit_bytes=55212 << 10
         ),
         name="sketch_histogram",
     )(grads, projection.T, bins, leaf.reshape(rows // 128, 128))

time: 39.3 us -> 37.8 us (0.962)
  local copies, waits for them, and re-layouts: 1.32 us -> 0.61 us
  Pallas kernels: 37.7 us -> 37.1 us
    unnamed x1, local copies, waits for them, and re-layouts: 1.32 us -> 0.61 us
    pallas_call x1, Pallas kernels: 37.7 us -> 37.1 us  [local(): pl.pallas_call(functools.partial(kernel, scale), out_shape=jax.ShapeDtype...]
where the time goes in v4:
time: 37.8 us; the launch traced here: 37.7 us
  Pallas kernels  37.1 us (98%)
  local copies, waits for them, and re-layouts  0.61 us (2%)
    pallas_call x1, Pallas kernels, local(): pl.pallas_call(functools.partial(kernel, scale), out_shape=jax.ShapeDtype...  37.1 us

profile of v4, /device:TPU:32, one launch (start us, length us, event | category | flops | bytes accessed | tf_op | source)
XLA Modules:
  0.0 37.7 jit_solution(9761795130414793170)
XLA Ops:
  0.0 37.1 %sketch_histogram.1 = f32[4,8,128]{2,1,0:T(8,128)S(1)} custom-call(bf16[6144,256]{1,0:T(8,128)(2,1)} %grads.1, bf16[8,1024]{1,0:T(8,128)(2,1)} %bitcast.5, s32[6144,256]{1,0:T(8,128)} %bins.1, s32[48,128]{1,0:T(8,128)} %bitcast.4), custom_call_target="tpu_custom_call" | custom-call | tf_op jit(solution)/shard_map/sketch_histogram/pallas_call | solution.py:354
  37.1 0.6 %copy.6 = f32[1,1,4,8,128]{4,3,2,1,0:T(8,128)} copy(f32[1,1,4,8,128]{4,3,2,1,0:T(8,128)S(1)} %bitcast.3) | data formatting | bytes 32768
